TPU v7x, 1024 devices: a whole 8x8x8 slice. The times are simulated.
1024 devices in a mesh: band: 16 (over y_hi, x), grid: 64 (over z, y_lo, core).
Axes of the slice: x: 8, y: 8 (y_hi: 2, y_lo: 4; y = y_hi * 4 + y_lo), z: 8, core: 2. Of those that a mesh axis runs over, the one named last changes fastest.
Arguments:
- resident: float32 [16, 128, 128, 128], P('band', 'grid'), may hold values from -2 to 2
- occupied: float32 [32, 128, 128, 128], P('band', 'grid'), may hold values from -2 to 2
Outputs:
- exchange_field: float32 [16, 128, 128, 128], P('band', 'grid')
All inputs are finite; a program needn't handle non-finite values.
Results may differ from a plain program's by a relative error of at most 0.0003.
Values sent between devices are 32-bit elements; how exact they have to be, the bound alone decides.
A program may use at most 32 MiB of HBM per device.

v0:
```python
import math

import jax
import jax.numpy as jnp
from jax import lax
from jax.sharding import PartitionSpec as P

NX = 128
NY = 128
NZ = 128
TURNS = 3


screening = 0.05
mix_fraction = 0.25
highest = lax.Precision.HIGHEST


def shifted(value, axis, steps):
    count = lax.axis_size(axis)
    pairs = [(source, (source + steps) % count) for source in range(count)]
    return lax.ppermute(value, axis, pairs)


def hartley_table(length):
    index = jnp.arange(length, dtype=jnp.int32)
    phase = index[:, None] * index[None, :] % length
    angle = phase.astype(jnp.float32) * (2.0 * math.pi / length)
    return jnp.cos(angle) + jnp.sin(angle)


def signed_freq(length, index):
    return jnp.minimum(index, length - index).astype(jnp.float32) * (2.0 * math.pi / length)


def coulomb_block(first_y, count_y):
    freq_x = signed_freq(NX, jnp.arange(NX, dtype=jnp.int32))
    freq_y = signed_freq(NY, first_y + jnp.arange(count_y, dtype=jnp.int32))
    freq_z = signed_freq(NZ, jnp.arange(NZ, dtype=jnp.int32))
    q_square = (
        freq_x[:, None, None] ** 2 + freq_y[None, :, None] ** 2 + freq_z[None, None, :] ** 2
    ) / (4.0 * screening**2)
    positive = q_square > 0
    safe_square = jnp.where(positive, q_square, jnp.ones_like(q_square))
    ratio = jnp.where(positive, -jnp.expm1(-safe_square) / safe_square, jnp.ones_like(q_square))
    return math.pi / screening**2 * ratio / (NX * NY * NZ)


def local(resident, occupied):
    width_y = NY // lax.axis_size("grid")
    kernel = coulomb_block(lax.axis_index("grid") * width_y, width_y)
    table_x = hartley_table(NX)
    table_y = hartley_table(NY)
    table_z = hartley_table(NZ)
    arrived = [occupied]
    visitors = occupied
    for turn_step in range(1, TURNS):
        visitors = shifted(visitors, "band", 1)
        arrived.append(visitors)
    accumulated = jnp.zeros(resident.shape, jnp.float32)
    for group_now in arrived:
        for visitor_slot in range(group_now.shape[0]):
            single = group_now[visitor_slot]
            along_z = jnp.einsum(
                "axyz,zk->axyk", single[None] * resident, table_z, precision=highest
            )
            modes = jnp.einsum(
                "axyz,xk->akyz",
                lax.all_to_all(
                    jnp.einsum("axyk,yl->axlk", along_z, table_y, precision=highest),
                    "grid",
                    split_axis=2,
                    concat_axis=1,
                    tiled=True,
                ),
                table_x,
                precision=highest,
            )
            filtered = modes * kernel[None]
            back_x = jnp.einsum("akyz,kx->axyz", filtered, table_x, precision=highest)
            slabs = lax.all_to_all(back_x, "grid", split_axis=1, concat_axis=2, tiled=True)
            back_y = jnp.einsum("axlz,ly->axyz", slabs, table_y, precision=highest)
            potential = jnp.einsum("axyk,kz->axyz", back_y, table_z, precision=highest)
            accumulated = accumulated + single[None] * potential
    return -mix_fraction * accumulated


def solution(mesh):
    placed = (P("band", "grid", None, None), P("band", "grid", None, None))
    return jax.shard_map(
        local, mesh=mesh, in_specs=placed, out_specs=P("band", "grid", None, None), check_vma=False
    )
```

profile of v0, /device:TPU:1, one launch (start us, length us, event | category | flops | bytes accessed | tf_op | source)
XLA Modules:
  0.0 224.3 jit_solution(13303289978908716336)
XLA Ops:
  0.0 3.9 %collective-permute-start = (f32[2,2,128,128]{3,2,1,0:T(8,128)}, f32[2,2,128,128]{3,2,1,0:T(8,128)S(1)}, u32[]{:S(2)}, u32[]{:S(2)}) collective-permute-start(f32[2,2,128,128]{3,2,1,0:T(8,128)} %param.3), channel_id=1, source_target_pairs={{0,64},{64,128},{128,192},{192,256},{256,320},{320,384},{384,448},... | collective-permute-start | bytes 786440 | tf_op jit(solution)/shard_map/ppermute | solution.py:22
  3.9 1.5 fusion.23
  6.8 21.7 %all-to-all-start = ((f32[1,2,128,128]{3,1,0,2:T(2,128)}), f32[1,2,128,128]{3,1,0,2:T(2,128)S(1)}, u32[]{:S(2)}, u32[]{:S(2)}) async-start(f32[1,2,128,128]{3,1,0,2:T(2,128)} %copy.58), calls=%async_computation | async-start | bytes 262144 | tf_op jit(solution)/shard_map/all_to_all | solution.py:69
  29.7 0.8 copy.66
  30.5 12.8 %all-to-all-done = f32[1,2,128,128]{3,1,0,2:T(2,128)S(1)} async-done(((f32[1,2,128,128]{3,1,0,2:T(2,128)}), f32[1,2,128,128]{3,1,0,2:T(2,128)S(1)}, u32[]{:S(2)}, u32[]{:S(2)}) %all-to-all-start) | async-done | bytes 131104 | tf_op jit(solution)/shard_map/all_to_all | solution.py:69
  43.3 7.0 %all-to-all-start.2 = ((f32[1,2,128,128]{3,1,0,2:T(2,128)}), f32[1,2,128,128]{3,1,0,2:T(2,128)S(1)}, u32[]{:S(2)}, u32[]{:S(2)}) async-start(f32[1,2,128,128]{3,1,0,2:T(2,128)} %copy.66), calls=%async_computation.2 | async-start | bytes 262144 | tf_op jit(solution)/shard_map/all_to_all | solution.py:69
  52.2 8.9 %all-to-all-done.2 = f32[1,2,128,128]{3,1,0,2:T(2,128)S(1)} async-done(((f32[1,2,128,128]{3,1,0,2:T(2,128)}), f32[1,2,128,128]{3,1,0,2:T(2,128)S(1)}, u32[]{:S(2)}, u32[]{:S(2)}) %all-to-all-start.2) | async-done | bytes 131104 | tf_op jit(solution)/shard_map/all_to_all | solution.py:69
  61.1 4.4 %all-to-all-start.1 = ((f32[1,128,2,128]{3,2,0,1:T(2,128)}), f32[1,128,2,128]{3,2,0,1:T(2,128)S(1)}, u32[]{:S(2)}, u32[]{:S(2)}) async-start(f32[1,128,2,128]{3,2,0,1:T(2,128)} %copy.62), calls=%async_computation.1 | async-start | bytes 262144 | tf_op jit(solution)/shard_map/all_to_all | solution.py:81
  68.6 0.8 copy.82
  69.4 7.1 %all-to-all-done.1 = f32[1,128,2,128]{3,2,0,1:T(2,128)S(1)} async-done(((f32[1,128,2,128]{3,2,0,1:T(2,128)}), f32[1,128,2,128]{3,2,0,1:T(2,128)S(1)}, u32[]{:S(2)}, u32[]{:S(2)}) %all-to-all-start.1) | async-done | bytes 131104 | tf_op jit(solution)/shard_map/all_to_all | solution.py:81
  76.5 4.4 %all-to-all-start.3 = ((f32[1,128,2,128]{3,2,0,1:T(2,128)}), f32[1,128,2,128]{3,2,0,1:T(2,128)S(1)}, u32[]{:S(2)}, u32[]{:S(2)}) async-start(f32[1,128,2,128]{3,2,0,1:T(2,128)} %copy.70), calls=%async_computation.3 | async-start | bytes 262144 | tf_op jit(solution)/shard_map/all_to_all | solution.py:81
  82.8 1.9 collective-permute-start.1
  84.7 7.1 %all-to-all-done.3 = f32[1,128,2,128]{3,2,0,1:T(2,128)S(1)} async-done(((f32[1,128,2,128]{3,2,0,1:T(2,128)}), f32[1,128,2,128]{3,2,0,1:T(2,128)S(1)}, u32[]{:S(2)}, u32[]{:S(2)}) %all-to-all-start.3) | async-done | bytes 131104 | tf_op jit(solution)/shard_map/all_to_all | solution.py:81
  91.8 4.5 %all-to-all-start.6 = ((f32[1,2,128,128]{3,1,0,2:T(2,128)}), f32[1,2,128,128]{3,1,0,2:T(2,128)S(1)}, u32[]{:S(2)}, u32[]{:S(2)}) async-start(f32[1,2,128,128]{3,1,0,2:T(2,128)} %copy.82), calls=%async_computation.6 | async-start | bytes 262144 | tf_op jit(solution)/shard_map/all_to_all | solution.py:69
  98.6 14.2 %all-to-all-done.6 = f32[1,2,128,128]{3,1,0,2:T(2,128)S(1)} async-done(((f32[1,2,128,128]{3,1,0,2:T(2,128)}), f32[1,2,128,128]{3,1,0,2:T(2,128)S(1)}, u32[]{:S(2)}, u32[]{:S(2)}) %all-to-all-start.6) | async-done | bytes 131104 | tf_op jit(solution)/shard_map/all_to_all | solution.py:69
  112.8 5.9 %all-to-all-start.4 = ((f32[1,2,128,128]{3,1,0,2:T(2,128)}), f32[1,2,128,128]{3,1,0,2:T(2,128)S(1)}, u32[]{:S(2)}, u32[]{:S(2)}) async-start(f32[1,2,128,128]{3,1,0,2:T(2,128)} %copy.74), calls=%async_computation.4 | async-start | bytes 262144 | tf_op jit(solution)/shard_map/all_to_all | solution.py:69
  119.9 0.8 copy.86
  120.6 8.9 %all-to-all-done.4 = f32[1,2,128,128]{3,1,0,2:T(2,128)S(1)} async-done(((f32[1,2,128,128]{3,1,0,2:T(2,128)}), f32[1,2,128,128]{3,1,0,2:T(2,128)S(1)}, u32[]{:S(2)}, u32[]{:S(2)}) %all-to-all-start.4) | async-done | bytes 131104 | tf_op jit(solution)/shard_map/all_to_all | solution.py:69
  129.5 4.4 %all-to-all-start.7 = ((f32[1,128,2,128]{3,2,0,1:T(2,128)}), f32[1,128,2,128]{3,2,0,1:T(2,128)S(1)}, u32[]{:S(2)}, u32[]{:S(2)}) async-start(f32[1,128,2,128]{3,2,0,1:T(2,128)} %copy.86), calls=%async_computation.7 | async-start | bytes 262144 | tf_op jit(solution)/shard_map/all_to_all | solution.py:81
  137.5 7.3 %all-to-all-done.7 = f32[1,128,2,128]{3,2,0,1:T(2,128)S(1)} async-done(((f32[1,128,2,128]{3,2,0,1:T(2,128)}), f32[1,128,2,128]{3,2,0,1:T(2,128)S(1)}, u32[]{:S(2)}, u32[]{:S(2)}) %all-to-all-start.7) | async-done | bytes 131104 | tf_op jit(solution)/shard_map/all_to_all | solution.py:81
  144.9 4.4 %all-to-all-start.5 = ((f32[1,128,2,128]{3,2,0,1:T(2,128)}), f32[1,128,2,128]{3,2,0,1:T(2,128)S(1)}, u32[]{:S(2)}, u32[]{:S(2)}) async-start(f32[1,128,2,128]{3,2,0,1:T(2,128)} %copy.78), calls=%async_computation.5 | async-start | bytes 262144 | tf_op jit(solution)/shard_map/all_to_all | solution.py:81
  152.0 8.2 %all-to-all-done.5 = f32[1,128,2,128]{3,2,0,1:T(2,128)S(1)} async-done(((f32[1,128,2,128]{3,2,0,1:T(2,128)}), f32[1,128,2,128]{3,2,0,1:T(2,128)S(1)}, u32[]{:S(2)}, u32[]{:S(2)}) %all-to-all-start.5) | async-done | bytes 131104 | tf_op jit(solution)/shard_map/all_to_all | solution.py:81
  160.2 4.4 %all-to-all-start.10 = ((f32[1,2,128,128]{3,1,0,2:T(2,128)}), f32[1,2,128,128]{3,1,0,2:T(2,128)S(1)}, u32[]{:S(2)}, u32[]{:S(2)}) async-start(f32[1,2,128,128]{3,1,0,2:T(2,128)} %copy.98), calls=%async_computation.10 | async-start | bytes 262144 | tf_op jit(solution)/shard_map/all_to_all | solution.py:69
  165.8 9.8 %all-to-all-done.10 = f32[1,2,128,128]{3,1,0,2:T(2,128)S(1)} async-done(((f32[1,2,128,128]{3,1,0,2:T(2,128)}), f32[1,2,128,128]{3,1,0,2:T(2,128)S(1)}, u32[]{:S(2)}, u32[]{:S(2)}) %all-to-all-start.10) | async-done | bytes 131104 | tf_op jit(solution)/shard_map/all_to_all | solution.py:69
  175.6 4.7 %all-to-all-start.8 = ((f32[1,2,128,128]{3,1,0,2:T(2,128)}), f32[1,2,128,128]{3,1,0,2:T(2,128)S(1)}, u32[]{:S(2)}, u32[]{:S(2)}) async-start(f32[1,2,128,128]{3,1,0,2:T(2,128)} %copy.90), calls=%async_computation.8 | async-start | bytes 262144 | tf_op jit(solution)/shard_map/all_to_all | solution.py:69
  181.5 0.8 copy.102
  182.2 9.0 %all-to-all-done.8 = f32[1,2,128,128]{3,1,0,2:T(2,128)S(1)} async-done(((f32[1,2,128,128]{3,1,0,2:T(2,128)}), f32[1,2,128,128]{3,1,0,2:T(2,128)S(1)}, u32[]{:S(2)}, u32[]{:S(2)}) %all-to-all-start.8) | async-done | bytes 131104 | tf_op jit(solution)/shard_map/all_to_all | solution.py:69
  191.2 4.4 %all-to-all-start.11 = ((f32[1,128,2,128]{3,2,0,1:T(2,128)}), f32[1,128,2,128]{3,2,0,1:T(2,128)S(1)}, u32[]{:S(2)}, u32[]{:S(2)}) async-start(f32[1,128,2,128]{3,2,0,1:T(2,128)} %copy.102), calls=%async_computation.11 | async-start | bytes 262144 | tf_op jit(solution)/shard_map/all_to_all | solution.py:81
  197.6 9.0 %all-to-all-done.11 = f32[1,128,2,128]{3,2,0,1:T(2,128)S(1)} async-done(((f32[1,128,2,128]{3,2,0,1:T(2,128)}), f32[1,128,2,128]{3,2,0,1:T(2,128)S(1)}, u32[]{:S(2)}, u32[]{:S(2)}) %all-to-all-start.11) | async-done | bytes 131104 | tf_op jit(solution)/shard_map/all_to_all | solution.py:81
  206.6 4.4 %all-to-all-start.9 = ((f32[1,128,2,128]{3,2,0,1:T(2,128)}), f32[1,128,2,128]{3,2,0,1:T(2,128)S(1)}, u32[]{:S(2)}, u32[]{:S(2)}) async-start(f32[1,128,2,128]{3,2,0,1:T(2,128)} %copy.94), calls=%async_computation.9 | async-start | bytes 262144 | tf_op jit(solution)/shard_map/all_to_all | solution.py:81
  212.2 9.8 %all-to-all-done.9 = f32[1,128,2,128]{3,2,0,1:T(2,128)S(1)} async-done(((f32[1,128,2,128]{3,2,0,1:T(2,128)}), f32[1,128,2,128]{3,2,0,1:T(2,128)S(1)}, u32[]{:S(2)}, u32[]{:S(2)}) %all-to-all-start.9) | async-done | bytes 131104 | tf_op jit(solution)/shard_map/all_to_all | solution.py:81
  223.1 1.2 fusion.10
  (63 shorter events, 25.4 us)
Async XLA Ops:
  0.0 67.5 %collective-permute-start = (f32[2,2,128,128]{3,2,1,0:T(8,128)}, f32[2,2,128,128]{3,2,1,0:T(8,128)S(1)}, u32[]{:S(2)}, u32[]{:S(2)}) collective-permute-start(f32[2,2,128,128]{3,2,1,0:T(8,128)} %param.3), channel_id=1, source_target_pairs={{0,64},{64,128},{128,192},{192,256},{256,320},{320,384},{384,448},... | collective-permute-start | bytes 786440 | tf_op jit(solution)/shard_map/ppermute | solution.py:22
  6.0 22.5 %copy-start.1 = (f32[2,2,128,128]{3,2,1,0:T(8,128)S(1)}, f32[2,2,128,128]{3,2,1,0:T(8,128)}, u32[]{:S(2)}) copy-start(f32[2,2,128,128]{3,2,1,0:T(8,128)} %param.3) | copy-start | bytes 786436
  6.8 21.7 %copy-start = (f32[1,2,128,128]{3,2,1,0:T(8,128)S(1)}, f32[1,2,128,128]{3,2,1,0:T(8,128)}, u32[]{:S(2)}) copy-start(f32[1,2,128,128]{3,2,1,0:T(8,128)} %param.2) | copy-start | bytes 393220
  6.8 36.5 %all-to-all-start = ((f32[1,2,128,128]{3,1,0,2:T(2,128)}), f32[1,2,128,128]{3,1,0,2:T(2,128)S(1)}, u32[]{:S(2)}, u32[]{:S(2)}) async-start(f32[1,2,128,128]{3,1,0,2:T(2,128)} %copy.58), calls=%async_computation | async-start | bytes 262144 | tf_op jit(solution)/shard_map/all_to_all | solution.py:69
  43.3 17.8 %all-to-all-start.2 = ((f32[1,2,128,128]{3,1,0,2:T(2,128)}), f32[1,2,128,128]{3,1,0,2:T(2,128)S(1)}, u32[]{:S(2)}, u32[]{:S(2)}) async-start(f32[1,2,128,128]{3,1,0,2:T(2,128)} %copy.66), calls=%async_computation.2 | async-start | bytes 262144 | tf_op jit(solution)/shard_map/all_to_all | solution.py:69
  61.1 15.4 %all-to-all-start.1 = ((f32[1,128,2,128]{3,2,0,1:T(2,128)}), f32[1,128,2,128]{3,2,0,1:T(2,128)S(1)}, u32[]{:S(2)}, u32[]{:S(2)}) async-start(f32[1,128,2,128]{3,2,0,1:T(2,128)} %copy.62), calls=%async_computation.1 | async-start | bytes 262144 | tf_op jit(solution)/shard_map/all_to_all | solution.py:81
  76.5 15.4 %all-to-all-start.3 = ((f32[1,128,2,128]{3,2,0,1:T(2,128)}), f32[1,128,2,128]{3,2,0,1:T(2,128)S(1)}, u32[]{:S(2)}, u32[]{:S(2)}) async-start(f32[1,128,2,128]{3,2,0,1:T(2,128)} %copy.70), calls=%async_computation.3 | async-start | bytes 262144 | tf_op jit(solution)/shard_map/all_to_all | solution.py:81
  82.8 53.1 %collective-permute-start.1 = (f32[2,2,128,128]{3,2,1,0:T(8,128)S(1)}, f32[2,2,128,128]{3,2,1,0:T(8,128)S(1)}, u32[]{:S(2)}, u32[]{:S(2)}) collective-permute-start(f32[2,2,128,128]{3,2,1,0:T(8,128)S(1)} %collective-permute-done), channel_id=1, source_target_pairs={{0,64},{64,128},{128,192},{192,256},{256,320},{320,384},{384,448},... | collective-permute-start | bytes 786440 | tf_op jit(solution)/shard_map/ppermute | solution.py:22
  91.8 20.9 %all-to-all-start.6 = ((f32[1,2,128,128]{3,1,0,2:T(2,128)}), f32[1,2,128,128]{3,1,0,2:T(2,128)S(1)}, u32[]{:S(2)}, u32[]{:S(2)}) async-start(f32[1,2,128,128]{3,1,0,2:T(2,128)} %copy.82), calls=%async_computation.6 | async-start | bytes 262144 | tf_op jit(solution)/shard_map/all_to_all | solution.py:69
  112.8 16.7 %all-to-all-start.4 = ((f32[1,2,128,128]{3,1,0,2:T(2,128)}), f32[1,2,128,128]{3,1,0,2:T(2,128)S(1)}, u32[]{:S(2)}, u32[]{:S(2)}) async-start(f32[1,2,128,128]{3,1,0,2:T(2,128)} %copy.74), calls=%async_computation.4 | async-start | bytes 262144 | tf_op jit(solution)/shard_map/all_to_all | solution.py:69
  129.5 15.4 %all-to-all-start.7 = ((f32[1,128,2,128]{3,2,0,1:T(2,128)}), f32[1,128,2,128]{3,2,0,1:T(2,128)S(1)}, u32[]{:S(2)}, u32[]{:S(2)}) async-start(f32[1,128,2,128]{3,2,0,1:T(2,128)} %copy.86), calls=%async_computation.7 | async-start | bytes 262144 | tf_op jit(solution)/shard_map/all_to_all | solution.py:81
  144.9 15.4 %all-to-all-start.5 = ((f32[1,128,2,128]{3,2,0,1:T(2,128)}), f32[1,128,2,128]{3,2,0,1:T(2,128)S(1)}, u32[]{:S(2)}, u32[]{:S(2)}) async-start(f32[1,128,2,128]{3,2,0,1:T(2,128)} %copy.78), calls=%async_computation.5 | async-start | bytes 262144 | tf_op jit(solution)/shard_map/all_to_all | solution.py:81
  160.2 15.4 %all-to-all-start.10 = ((f32[1,2,128,128]{3,1,0,2:T(2,128)}), f32[1,2,128,128]{3,1,0,2:T(2,128)S(1)}, u32[]{:S(2)}, u32[]{:S(2)}) async-start(f32[1,2,128,128]{3,1,0,2:T(2,128)} %copy.98), calls=%async_computation.10 | async-start | bytes 262144 | tf_op jit(solution)/shard_map/all_to_all | solution.py:69
  175.6 15.6 %all-to-all-start.8 = ((f32[1,2,128,128]{3,1,0,2:T(2,128)}), f32[1,2,128,128]{3,1,0,2:T(2,128)S(1)}, u32[]{:S(2)}, u32[]{:S(2)}) async-start(f32[1,2,128,128]{3,1,0,2:T(2,128)} %copy.90), calls=%async_computation.8 | async-start | bytes 262144 | tf_op jit(solution)/shard_map/all_to_all | solution.py:69
  191.2 15.4 %all-to-all-start.11 = ((f32[1,128,2,128]{3,2,0,1:T(2,128)}), f32[1,128,2,128]{3,2,0,1:T(2,128)S(1)}, u32[]{:S(2)}, u32[]{:S(2)}) async-start(f32[1,128,2,128]{3,2,0,1:T(2,128)} %copy.102), calls=%async_computation.11 | async-start | bytes 262144 | tf_op jit(solution)/shard_map/all_to_all | solution.py:81
  206.6 15.4 %all-to-all-start.9 = ((f32[1,128,2,128]{3,2,0,1:T(2,128)}), f32[1,128,2,128]{3,2,0,1:T(2,128)S(1)}, u32[]{:S(2)}, u32[]{:S(2)}) async-start(f32[1,128,2,128]{3,2,0,1:T(2,128)} %copy.94), calls=%async_computation.9 | async-start | bytes 262144 | tf_op jit(solution)/shard_map/all_to_all | solution.py:81
where the time goes:
time: 225 us; the launch traced here: 224 us
  waiting for transfers between devices  112 us (50%)
  starting transfers between devices  80.6 us (36%)
  matrix products  21.5 us (10%)
  local copies, waits for them, and re-layouts  9.59 us (4%)
    all_to_all x6, waiting for transfers between devices, local(): lax.all_to_all(jnp.einsum('axyk,yl->axlk', along_z, table_y, precision=hi...  63.5 us
    all_to_all x6, waiting for transfers between devices, local(): lax.all_to_all(back_x, 'grid', split_axis=1, concat_axis=2, tiled=True)  48.5 us
    all_to_all x6, starting transfers between devices, local(): lax.all_to_all(jnp.einsum('axyk,yl->axlk', along_z, table_y, precision=hi...  48.1 us
    all_to_all x6, starting transfers between devices, local(): lax.all_to_all(back_x, 'grid', split_axis=1, concat_axis=2, tiled=True)  26.6 us
    ppermute x2, starting transfers between devices, shifted(): return lax.ppermute(value, axis, pairs)  5.84 us
    transpose x6, local copies, waits for them, and re-layouts, local(): back_x = jnp.einsum('akyz,kx->axyz', filtered, table_x, precision=highest)  4.51 us
    transpose x6, local copies, waits for them, and re-layouts, local(): jnp.einsum('axyk,yl->axlk', along_z, table_y, precision=highest)  4.51 us
  transfers between devices with their start and end apart: 14, of which 12 were waited for; matrix products, arithmetic and copies ran while one was open for 13% of the time, Pallas kernels for 0%

commit v1 on v0

v1 whole, which is shorter than its diff:
```python
import functools
import math

import jax
import jax.numpy as jnp
import numpy as np
from jax import lax
from jax.experimental import pallas as pl
from jax.experimental.pallas import tpu as pltpu
from jax.sharding import PartitionSpec as P

N = 128
CELLS = N * N * N
TURNS = 3
BANDS = 16
GRID = 64
screening = 0.05
mix_fraction = 0.25
MESH = pl.DeviceIdType.MESH
F32 = jnp.float32
BF16 = jnp.bfloat16


def split_table(table):
    high = table.astype(np.float32).astype(jnp.bfloat16)
    low = (table - high.astype(np.float64)).astype(np.float32).astype(jnp.bfloat16)
    return [high, low]


def tables():
    index = np.arange(N)
    angle = (index[:, None] * index[None, :] % N) * (2.0 * math.pi / N)
    cas = np.cos(angle) + np.sin(angle)
    along_z = np.kron(np.eye(2), cas)
    along_y = np.zeros((N // 4, 2, 4, 2, N))
    for plane in range(2):
        along_y[:, plane, :, plane, :] = cas.reshape(N // 4, 4, N)
    along_y = along_y.reshape(2 * N, 2 * N)
    out = []
    for table in (along_z, along_y, along_y.T, cas):
        out += split_table(table)
    return out


def halves(value):
    high = value.astype(BF16)
    low = (value - high.astype(F32)).astype(BF16)
    return high, low


def dot(a, b):
    return jnp.dot(a, b, preferred_element_type=F32)


def data_by_table(value, high, low):
    a, b = halves(value)
    return dot(a, high[...]) + (dot(b, high[...]) + dot(a, low[...]))


def table_by_data(high, low, value):
    a, b = halves(value)
    return dot(high[...], a) + (dot(high[...], b) + dot(low[...], a))


def signed_square(index):
    signed = jnp.minimum(index, N - index).astype(F32) * (2.0 * math.pi / N)
    return signed * signed


def kernel(
    res, occ, z_high, z_low, y_high, y_low, yt_high, yt_low, x_high, x_low, out,
    visit, sbuf, rbuf, sback, rback, coef,
    visit_send, visit_recv, send_sem, recv_sem, bsend_sem, brecv_sem,
):
    band = lax.axis_index("band")
    me = lax.axis_index("grid")
    mine = pl.ds(pl.multiple_of(me * 8, 8), 8)

    barrier = pltpu.get_barrier_semaphore()

    def greet(step, carry):
        pl.semaphore_signal(
            barrier, inc=1, device_id={"grid": lax.rem(me + step, GRID)}, device_id_type=MESH
        )
        return carry

    lax.fori_loop(1, GRID, greet, 0)
    for shift in (1, 2, BANDS - 2, BANDS - 1):
        pl.semaphore_signal(
            barrier, inc=1, device_id={"band": lax.rem(band + shift, BANDS)}, device_id_type=MESH
        )

    def visitors(turn):
        return occ if turn == 0 else visit.at[turn - 1]

    def forward(turn):
        orbital = res[0].reshape(2 * N, N)
        group = visitors(turn)
        pair = jnp.concatenate([group[v].reshape(2 * N, N) * orbital for v in range(2)], axis=1)
        along_z = data_by_table(pair, z_high, z_low)
        modes = table_by_data(y_high, y_low, along_z)
        for v in range(2):
            sbuf[turn, :, v] = modes[:, v * N : (v + 1) * N].reshape(N // 4, 8, N)

    def each_peer(start_copy):
        start_copy(lax.rem(me + GRID // 2, GRID))

        def step(index, carry):
            offset = GRID // 2 - index
            start_copy(lax.rem(me + offset, GRID))
            start_copy(lax.rem(me + (GRID - offset), GRID))
            return carry

        lax.fori_loop(1, GRID // 2, step, 0)

    def send(turn):
        def start_copy(peer):
            pltpu.make_async_remote_copy(
                src_ref=sbuf.at[turn, lax.div(peer, 2), lax.rem(peer, 2)],
                dst_ref=rbuf.at[turn, mine],
                send_sem=send_sem.at[turn],
                recv_sem=recv_sem.at[turn],
                device_id={"grid": peer},
                device_id_type=MESH,
            ).start()

        each_peer(start_copy)
        rbuf[turn, mine] = sbuf[turn, lax.div(me, 2), lax.rem(me, 2)]

    def send_back(turn):
        def start_copy(peer):
            pltpu.make_async_remote_copy(
                src_ref=sback.at[turn, pl.ds(pl.multiple_of(peer * 8, 8), 8)],
                dst_ref=rback.at[turn, lax.div(me, 2), lax.rem(me, 2)],
                send_sem=bsend_sem.at[turn],
                recv_sem=brecv_sem.at[turn],
                device_id={"grid": peer},
                device_id_type=MESH,
            ).start()

        each_peer(start_copy)
        rback[turn, lax.div(me, 2), lax.rem(me, 2)] = sback[turn, mine]

    def wait_all(sem):
        part = rbuf.at[0, pl.ds(0, (GRID - 1) * 8)]
        pltpu.make_async_copy(part, part, sem).wait()

    def columns(turn):
        wait_all(recv_sem.at[turn])
        value = jnp.concatenate(
            [rbuf[turn, pl.ds(row, N, stride=4), :] for row in range(4)], axis=1
        )
        modes = table_by_data(x_high, x_low, value) * coef[...]
        back = table_by_data(x_high, x_low, modes)
        for row in range(4):
            sback[turn, pl.ds(row, N, stride=4), :] = back[:, row * N : (row + 1) * N]

    def inverse(turn):
        wait_all(brecv_sem.at[turn])
        value = jnp.concatenate([rback[turn, :, v].reshape(2 * N, N) for v in range(2)], axis=1)
        along_y = table_by_data(yt_high, yt_low, value)
        potential = data_by_table(along_y, z_high, z_low)
        group = visitors(turn)
        term = group[0].reshape(2 * N, N) * potential[:, :N]
        return term + group[1].reshape(2 * N, N) * potential[:, N:]

    first = lax.div(me, 2) * 4
    square_x = signed_square(lax.broadcasted_iota(jnp.int32, (N, N), 0))
    square_z = signed_square(lax.broadcasted_iota(jnp.int32, (N, N), 1))
    for row in range(4):
        square_y = signed_square(jnp.full((N, N), first + row, jnp.int32))
        q_square = (square_x + square_y + square_z) / (4.0 * screening**2)
        positive = q_square > 0
        safe = jnp.where(positive, q_square, 1.0)
        ratio = jnp.where(positive, (1.0 - jnp.exp(-safe)) / safe, 1.0)
        coef[:, row * N : (row + 1) * N] = (math.pi / screening**2 / CELLS) * ratio
    forward(0)

    pl.semaphore_wait(barrier, GRID - 1 + 4)

    visits = []
    for shift in (1, 2):
        copy = pltpu.make_async_remote_copy(
            src_ref=occ,
            dst_ref=visit.at[shift - 1],
            send_sem=visit_send.at[shift - 1],
            recv_sem=visit_recv.at[shift - 1],
            device_id={"band": lax.rem(band + shift, BANDS)},
            device_id_type=MESH,
        )
        copy.start()
        visits.append(copy)
    send(0)
    visits[0].wait_recv()
    forward(1)
    send(1)
    columns(0)
    send_back(0)
    visits[1].wait_recv()
    forward(2)
    send(2)
    columns(1)
    send_back(1)
    columns(2)
    send_back(2)
    total = inverse(0)
    total = total + inverse(1)
    total = total + inverse(2)
    out[0] = total.reshape(2, N, N)

    for copy in visits:
        copy.wait_send()
    for turn in range(TURNS):
        wait_all(send_sem.at[turn])
        wait_all(bsend_sem.at[turn])


def local(resident, occupied):
    vmem = pl.BlockSpec(memory_space=pltpu.VMEM)
    total = pl.pallas_call(
        kernel,
        out_shape=jax.ShapeDtypeStruct((1, 2, N, N), F32),
        in_specs=[vmem] * 10,
        out_specs=vmem,
        scratch_shapes=[
            pltpu.VMEM((TURNS - 1, 2, 2, N, N), F32),
            pltpu.VMEM((TURNS, GRID // 2, 2, 8, N), F32),
            pltpu.VMEM((TURNS, GRID * 8, N), F32),
            pltpu.VMEM((TURNS, GRID * 8, N), F32),
            pltpu.VMEM((TURNS, GRID // 2, 2, 8, N), F32),
            pltpu.VMEM((N, 4 * N), F32),
            pltpu.SemaphoreType.DMA((TURNS - 1,)),
            pltpu.SemaphoreType.DMA((TURNS - 1,)),
            pltpu.SemaphoreType.DMA((TURNS,)),
            pltpu.SemaphoreType.DMA((TURNS,)),
            pltpu.SemaphoreType.DMA((TURNS,)),
            pltpu.SemaphoreType.DMA((TURNS,)),
        ],
        compiler_params=pltpu.CompilerParams(collective_id=0, has_side_effects=True),
    )(resident, occupied, *[jnp.asarray(table) for table in tables()])
    return -mix_fraction * total


def solution(mesh):
    spec = P("band", "grid", None, None)
    return jax.shard_map(local, mesh=mesh, in_specs=(spec, spec), out_specs=spec, check_vma=False)
```

time: 225 us -> 90.6 us (0.40)
  waiting for transfers between devices: 112 us -> 0 us
  Pallas kernels: 0 us -> 88.9 us
  starting transfers between devices: 80.6 us -> 0 us
  matrix products: 21.5 us -> 0 us
  local copies, waits for them, and re-layouts: 9.59 us -> 0 us
    all_to_all x12 -> x0, waiting for transfers between devices: 112 us -> none  [the longest x6 63.5 us: local(): lax.all_to_all(jnp.einsum('axyk,yl->axlk', along_z, table_y, precision=hi...]
    pallas_call x0 -> x1, Pallas kernels: none -> 88.9 us  [local(): pl.pallas_call(kernel, out_shape=jax.ShapeDtypeStruct((1, 2, N, N), F32),...]
    all_to_all x12 -> x0, starting transfers between devices: 74.8 us -> none  [the longest x6 48.1 us: local(): lax.all_to_all(jnp.einsum('axyk,yl->axlk', along_z, table_y, precision=hi...]
    dot_general x36 -> x0, matrix products: 21.5 us -> none  [the longest x6 4.17 us: local(): jnp.einsum('axyz,zk->axyk', single[None] * resident, table_z, precision=h...]
    transpose x12 -> x0, local copies, waits for them, and re-layouts: 9.02 us -> none  [the longest x6 4.51 us: local(): back_x = jnp.einsum('akyz,kx->axyz', filtered, table_x, precision=highest)]
    ppermute x2 -> x0, starting transfers between devices: 5.84 us -> none  [shifted(): return lax.ppermute(value, axis, pairs)]
  transfers between devices with their start and end apart: 14 -> 0, of which waited for: 12 -> 0; matrix products, arithmetic and copies ran while one was open for 13% -> 0% of each run, Pallas kernels for 0% -> 0%
where the time goes in v1:
time: 90.6 us; the launch traced here: 90.5 us
  Pallas kernels  88.9 us (98%)
  other arithmetic  1.57 us (2%)
    pallas_call x1, Pallas kernels, local(): pl.pallas_call(kernel, out_shape=jax.ShapeDtypeStruct((1, 2, N, N), F32),...  88.9 us

profile of v1, /device:TPU:1, one launch (start us, length us, event | category | flops | bytes accessed | tf_op | source)
XLA Modules:
  0.0 90.5 jit_solution(4739177827647383812)
XLA Ops:
  0.0 88.9 %shard_map.100 = f32[1,2,128,128]{3,2,1,0:T(8,128)} custom-call(f32[1,2,128,128]{3,2,1,0:T(8,128)} %res.1, f32[2,2,128,128]{3,2,1,0:T(8,128)} %occ.1, bf16[256,256]{1,0:T(8,128)(2,1)} %constant.18.clone.z_high, bf16[256,256]{1,0:T(8,128)(2,1)} %constant.19.clone.z_low, bf16[256,256]{1,0:T(8,128)(2,1)} %constant.20.clone.y_high, ...), custom_call_target="tpu_custom_call" | custom-call | tf_op jit(solution)/shard_map/pallas_call | solution.py:220
  88.9 1.6 %broadcast_multiply_fusion = f32[1,2,128,128]{3,2,1,0:T(8,128)} fusion(f32[1,2,128,128]{3,2,1,0:T(8,128)} %shard_map.100), kind=kLoop, calls=%fused_computation | loop fusion | flops 32768 | bytes 262144 | tf_op jit(solution)/shard_map/mul | solution.py:241

commit v2 on v1

--- a/solution.py
+++ b/solution.py
@@ -14,6 +14,8 @@
 TURNS = 3
 BANDS = 16
 GRID = 64
+LINE = 8
+PIECE = N // LINE
 screening = 0.05
 mix_fraction = 0.25
 MESH = pl.DeviceIdType.MESH
@@ -69,8 +71,8 @@
 
 def kernel(
     res, occ, z_high, z_low, y_high, y_low, yt_high, yt_low, x_high, x_low, out,
-    visit, sbuf, rbuf, sback, rback, coef,
-    visit_send, visit_recv, send_sem, recv_sem, bsend_sem, brecv_sem,
+    visit, cross, sbuf, rbuf, sback, rback, coef,
+    visit_send, visit_recv, cross_send, cross_recv, pass_send, send_sem, recv_sem, bsend_sem, brecv_sem,
 ):
     band = lax.axis_index("band")
     me = lax.axis_index("grid")
@@ -85,10 +87,14 @@
         return carry
 
     lax.fori_loop(1, GRID, greet, 0)
-    for shift in (1, 2, BANDS - 2, BANDS - 1):
+
+    def greet_band(step, carry):
         pl.semaphore_signal(
-            barrier, inc=1, device_id={"band": lax.rem(band + shift, BANDS)}, device_id_type=MESH
+            barrier, inc=1, device_id={"band": lax.rem(band + step, BANDS)}, device_id_type=MESH
         )
+        return carry
+
+    lax.fori_loop(1, BANDS, greet_band, 0)
 
     def visitors(turn):
         return occ if turn == 0 else visit.at[turn - 1]
@@ -176,29 +182,93 @@
         coef[:, row * N : (row + 1) * N] = (math.pi / screening**2 / CELLS) * ratio
     forward(0)
 
-    pl.semaphore_wait(barrier, GRID - 1 + 4)
-
-    visits = []
-    for shift in (1, 2):
-        copy = pltpu.make_async_remote_copy(
+    pl.semaphore_wait(barrier, GRID - 1 + BANDS - 1)
+
+    place = lax.rem(band, LINE)
+    side = lax.div(band, LINE)
+    whole = visit.at[0]
+
+    def shift_copy(shift):
+        return pltpu.make_async_remote_copy(
             src_ref=occ,
             dst_ref=visit.at[shift - 1],
             send_sem=visit_send.at[shift - 1],
             recv_sem=visit_recv.at[shift - 1],
-            device_id={"band": lax.rem(band + shift, BANDS)},
+            device_id={"band": band + shift},
             device_id_type=MESH,
         )
-        copy.start()
-        visits.append(copy)
+
+    def piece(index):
+        return pl.ds(pl.multiple_of(index * PIECE, PIECE), PIECE)
+
+    for late in range(2):
+        @pl.when(place == LINE - 1 - late)
+        def _():
+            def step(index, carry):
+                pltpu.make_async_remote_copy(
+                    src_ref=occ.at[:, :, piece(index)],
+                    dst_ref=cross.at[late],
+                    send_sem=cross_send.at[late],
+                    recv_sem=cross_recv.at[late],
+                    device_id={"band": (1 - side) * LINE + index},
+                    device_id_type=MESH,
+                ).start()
+                return carry
+
+            lax.fori_loop(0, LINE, step, 0)
+
+    for shift in (1, 2):
+        @pl.when(place + shift < LINE)
+        def _():
+            shift_copy(shift).start()
+
+    def pass_on(late, target, slot, order):
+        part = visit.at[slot, :, :, piece(place)]
+
+        @pl.when(place == target)
+        def _():
+            pltpu.make_async_copy(cross.at[late], part, visit_recv.at[slot]).start()
+
+        @pl.when(place != target)
+        def _():
+            pltpu.make_async_remote_copy(
+                src_ref=cross.at[late],
+                dst_ref=part,
+                send_sem=pass_send.at[order],
+                recv_sem=visit_recv.at[slot],
+                device_id={"band": side * LINE + target},
+                device_id_type=MESH,
+            ).start()
+
+    passes = ((0, 0, 0), (0, 1, 1), (1, 0, 1))
+
+    def relay():
+        pltpu.make_async_copy(cross.at[0], cross.at[0], cross_recv.at[0]).wait()
+        pass_on(*passes[0], 0)
+        pass_on(*passes[1], 1)
+        pltpu.make_async_copy(cross.at[1], cross.at[1], cross_recv.at[1]).wait()
+        pass_on(*passes[2], 2)
+
+    def next_turn(turn):
+        pltpu.make_async_copy(whole, whole, visit_recv.at[turn - 1]).wait()
+        forward(turn)
+        send(turn)
+
     send(0)
-    visits[0].wait_recv()
-    forward(1)
-    send(1)
+    relay()
+
+    @pl.when(place > 0)
+    def _():
+        next_turn(1)
+
     columns(0)
     send_back(0)
-    visits[1].wait_recv()
-    forward(2)
-    send(2)
+
+    @pl.when(place == 0)
+    def _():
+        next_turn(1)
+
+    next_turn(2)
     columns(1)
     send_back(1)
     columns(2)
@@ -208,8 +278,21 @@
     total = total + inverse(2)
     out[0] = total.reshape(2, N, N)
 
-    for copy in visits:
-        copy.wait_send()
+    for shift in (1, 2):
+        @pl.when(place + shift < LINE)
+        def _():
+            shift_copy(shift).wait_send()
+
+    for late in range(2):
+        @pl.when(place == LINE - 1 - late)
+        def _():
+            pltpu.make_async_copy(whole, whole, cross_send.at[late]).wait()
+
+    for order, (late, target, slot) in enumerate(passes):
+        @pl.when(place != target)
+        def _():
+            pltpu.make_async_copy(cross.at[late], cross.at[late], pass_send.at[order]).wait()
+
     for turn in range(TURNS):
         wait_all(send_sem.at[turn])
         wait_all(bsend_sem.at[turn])
@@ -224,6 +307,7 @@
         out_specs=vmem,
         scratch_shapes=[
             pltpu.VMEM((TURNS - 1, 2, 2, N, N), F32),
+            pltpu.VMEM((2, 2, 2, PIECE, N), F32),
             pltpu.VMEM((TURNS, GRID // 2, 2, 8, N), F32),
             pltpu.VMEM((TURNS, GRID * 8, N), F32),
             pltpu.VMEM((TURNS, GRID * 8, N), F32),
@@ -231,6 +315,9 @@
             pltpu.VMEM((N, 4 * N), F32),
             pltpu.SemaphoreType.DMA((TURNS - 1,)),
             pltpu.SemaphoreType.DMA((TURNS - 1,)),
+            pltpu.SemaphoreType.DMA((2,)),
+            pltpu.SemaphoreType.DMA((2,)),
+            pltpu.SemaphoreType.DMA((3,)),
             pltpu.SemaphoreType.DMA((TURNS,)),
             pltpu.SemaphoreType.DMA((TURNS,)),
             pltpu.SemaphoreType.DMA((TURNS,)),

time: 90.6 us -> 77.7 us (0.86)
  Pallas kernels: 88.9 us -> 76 us
    pallas_call x1, Pallas kernels: 88.9 us -> 76 us  [local(): pl.pallas_call(kernel, out_shape=jax.ShapeDtypeStruct((1, 2, N, N), F32),...]
where the time goes in v2:
time: 77.7 us; the launch traced here: 77.5 us
  Pallas kernels  76 us (98%)
  other arithmetic  1.57 us (2%)
    pallas_call x1, Pallas kernels, local(): pl.pallas_call(kernel, out_shape=jax.ShapeDtypeStruct((1, 2, N, N), F32),...  76 us
    mul x1, other arithmetic, local(): return -mix_fraction * total  1.57 us

profile of v2, /device:TPU:1, one launch (start us, length us, event | category | flops | bytes accessed | tf_op | source)
XLA Modules:
  0.0 77.5 jit_solution(11225356859663409435)
XLA Ops:
  0.0 76.0 %shard_map.100 = f32[1,2,128,128]{3,2,1,0:T(8,128)} custom-call(f32[1,2,128,128]{3,2,1,0:T(8,128)} %res.1, f32[2,2,128,128]{3,2,1,0:T(8,128)} %occ.1, bf16[256,256]{1,0:T(8,128)(2,1)} %constant.18.clone.z_high, bf16[256,256]{1,0:T(8,128)(2,1)} %constant.19.clone.z_low, bf16[256,256]{1,0:T(8,128)(2,1)} %constant.20.clone.y_high, ...), custom_call_target="tpu_custom_call" | custom-call | tf_op jit(solution)/shard_map/pallas_call | solution.py:303
  76.0 1.6 %broadcast_multiply_fusion = f32[1,2,128,128]{3,2,1,0:T(8,128)} fusion(f32[1,2,128,128]{3,2,1,0:T(8,128)} %shard_map.100), kind=kLoop, calls=%fused_computation | loop fusion | flops 32768 | bytes 262144 | tf_op jit(solution)/shard_map/mul | solution.py:328

commit v3 on v2

--- a/solution.py
+++ b/solution.py
@@ -151,6 +151,18 @@
         part = rbuf.at[0, pl.ds(0, (GRID - 1) * 8)]
         pltpu.make_async_copy(part, part, sem).wait()
 
+    def factors():
+        first = lax.div(me, 2) * 4
+        square_x = signed_square(lax.broadcasted_iota(jnp.int32, (N, N), 0))
+        square_z = signed_square(lax.broadcasted_iota(jnp.int32, (N, N), 1))
+        for row in range(4):
+            square_y = signed_square(jnp.full((N, N), first + row, jnp.int32))
+            q_square = (square_x + square_y + square_z) / (4.0 * screening**2)
+            positive = q_square > 0
+            safe = jnp.where(positive, q_square, 1.0)
+            ratio = jnp.where(positive, (1.0 - jnp.exp(-safe)) / safe, 1.0)
+            coef[:, row * N : (row + 1) * N] = (math.pi / screening**2 / CELLS) * ratio
+
     def columns(turn):
         wait_all(recv_sem.at[turn])
         value = jnp.concatenate(
@@ -170,16 +182,6 @@
         term = group[0].reshape(2 * N, N) * potential[:, :N]
         return term + group[1].reshape(2 * N, N) * potential[:, N:]
 
-    first = lax.div(me, 2) * 4
-    square_x = signed_square(lax.broadcasted_iota(jnp.int32, (N, N), 0))
-    square_z = signed_square(lax.broadcasted_iota(jnp.int32, (N, N), 1))
-    for row in range(4):
-        square_y = signed_square(jnp.full((N, N), first + row, jnp.int32))
-        q_square = (square_x + square_y + square_z) / (4.0 * screening**2)
-        positive = q_square > 0
-        safe = jnp.where(positive, q_square, 1.0)
-        ratio = jnp.where(positive, (1.0 - jnp.exp(-safe)) / safe, 1.0)
-        coef[:, row * N : (row + 1) * N] = (math.pi / screening**2 / CELLS) * ratio
     forward(0)
 
     pl.semaphore_wait(barrier, GRID - 1 + BANDS - 1)
@@ -188,15 +190,19 @@
     side = lax.div(band, LINE)
     whole = visit.at[0]
 
-    def shift_copy(shift):
+    def hand_on(source, slot):
         return pltpu.make_async_remote_copy(
-            src_ref=occ,
-            dst_ref=visit.at[shift - 1],
-            send_sem=visit_send.at[shift - 1],
-            recv_sem=visit_recv.at[shift - 1],
-            device_id={"band": band + shift},
+            src_ref=source,
+            dst_ref=visit.at[slot],
+            send_sem=visit_send.at[slot],
+            recv_sem=visit_recv.at[slot],
+            device_id={"band": band + 1},
             device_id_type=MESH,
         )
+
+    first_hand = hand_on(occ, 0)
+    second_hand = hand_on(visit.at[0], 1)
+    inner = jnp.logical_and(place > 0, place < LINE - 1)
 
     def piece(index):
         return pl.ds(pl.multiple_of(index * PIECE, PIECE), PIECE)
@@ -217,10 +223,9 @@
 
             lax.fori_loop(0, LINE, step, 0)
 
-    for shift in (1, 2):
-        @pl.when(place + shift < LINE)
-        def _():
-            shift_copy(shift).start()
+    @pl.when(place < LINE - 1)
+    def _():
+        first_hand.start()
 
     def pass_on(late, target, slot, order):
         part = visit.at[slot, :, :, piece(place)]
@@ -240,14 +245,11 @@
                 device_id_type=MESH,
             ).start()
 
-    passes = ((0, 0, 0), (0, 1, 1), (1, 0, 1))
-
-    def relay():
-        pltpu.make_async_copy(cross.at[0], cross.at[0], cross_recv.at[0]).wait()
-        pass_on(*passes[0], 0)
-        pass_on(*passes[1], 1)
-        pltpu.make_async_copy(cross.at[1], cross.at[1], cross_recv.at[1]).wait()
-        pass_on(*passes[2], 2)
+    passes = ((0, 0, 0), (1, 0, 1), (0, 1, 1))
+
+    def relay(late):
+        pltpu.make_async_copy(cross.at[late], cross.at[late], cross_recv.at[late]).wait()
+        pass_on(*passes[late], late)
 
     def next_turn(turn):
         pltpu.make_async_copy(whole, whole, visit_recv.at[turn - 1]).wait()
@@ -255,11 +257,19 @@
         send(turn)
 
     send(0)
-    relay()
+    factors()
+    relay(0)
 
     @pl.when(place > 0)
     def _():
         next_turn(1)
+
+    relay(1)
+    pass_on(*passes[2], 2)
+
+    @pl.when(inner)
+    def _():
+        second_hand.start()
 
     columns(0)
     send_back(0)
@@ -278,10 +288,13 @@
     total = total + inverse(2)
     out[0] = total.reshape(2, N, N)
 
-    for shift in (1, 2):
-        @pl.when(place + shift < LINE)
-        def _():
-            shift_copy(shift).wait_send()
+    @pl.when(place < LINE - 1)
+    def _():
+        first_hand.wait_send()
+
+    @pl.when(inner)
+    def _():
+        second_hand.wait_send()
 
     for late in range(2):
         @pl.when(place == LINE - 1 - late)

time: 77.7 us -> 75 us (0.965)
  Pallas kernels: 76 us -> 73.2 us
    pallas_call x1, Pallas kernels: 76 us -> 73.2 us  [local(): pl.pallas_call(kernel, out_shape=jax.ShapeDtypeStruct((1, 2, N, N), F32),...]
where the time goes in v3:
time: 75 us; the launch traced here: 74.8 us
  Pallas kernels  73.2 us (98%)
  other arithmetic  1.57 us (2%)
    pallas_call x1, Pallas kernels, local(): pl.pallas_call(kernel, out_shape=jax.ShapeDtypeStruct((1, 2, N, N), F32),...  73.2 us
    mul x1, other arithmetic, local(): return -mix_fraction * total  1.57 us

profile of v3, /device:TPU:1, one launch (start us, length us, event | category | flops | bytes accessed | tf_op | source)
XLA Modules:
  0.0 74.8 jit_solution(2656484055449308247)
XLA Ops:
  0.0 73.2 %shard_map.100 = f32[1,2,128,128]{3,2,1,0:T(8,128)} custom-call(f32[1,2,128,128]{3,2,1,0:T(8,128)} %res.1, f32[2,2,128,128]{3,2,1,0:T(8,128)} %occ.1, bf16[256,256]{1,0:T(8,128)(2,1)} %constant.18.clone.z_high, bf16[256,256]{1,0:T(8,128)(2,1)} %constant.19.clone.z_low, bf16[256,256]{1,0:T(8,128)(2,1)} %constant.20.clone.y_high, ...), custom_call_target="tpu_custom_call" | custom-call | tf_op jit(solution)/shard_map/pallas_call | solution.py:316
  73.2 1.6 %broadcast_multiply_fusion = f32[1,2,128,128]{3,2,1,0:T(8,128)} fusion(f32[1,2,128,128]{3,2,1,0:T(8,128)} %shard_map.100), kind=kLoop, calls=%fused_computation | loop fusion | flops 32768 | bytes 262144 | tf_op jit(solution)/shard_map/mul | solution.py:341

commit v4 on v3

--- a/solution.py
+++ b/solution.py
@@ -15,7 +15,9 @@
 BANDS = 16
 GRID = 64
 LINE = 8
-PIECE = N // LINE
+VIA = 2
+VIAS = 4
+PIECE = N // VIAS
 screening = 0.05
 mix_fraction = 0.25
 MESH = pl.DeviceIdType.MESH
@@ -216,34 +218,28 @@
                     dst_ref=cross.at[late],
                     send_sem=cross_send.at[late],
                     recv_sem=cross_recv.at[late],
-                    device_id={"band": (1 - side) * LINE + index},
+                    device_id={"band": (1 - side) * LINE + VIA + index},
                     device_id_type=MESH,
                 ).start()
                 return carry
 
-            lax.fori_loop(0, LINE, step, 0)
+            lax.fori_loop(0, VIAS, step, 0)
 
     @pl.when(place < LINE - 1)
     def _():
         first_hand.start()
 
+    via = jnp.logical_and(place >= VIA, place < VIA + VIAS)
+
     def pass_on(late, target, slot, order):
-        part = visit.at[slot, :, :, piece(place)]
-
-        @pl.when(place == target)
-        def _():
-            pltpu.make_async_copy(cross.at[late], part, visit_recv.at[slot]).start()
-
-        @pl.when(place != target)
-        def _():
-            pltpu.make_async_remote_copy(
-                src_ref=cross.at[late],
-                dst_ref=part,
-                send_sem=pass_send.at[order],
-                recv_sem=visit_recv.at[slot],
-                device_id={"band": side * LINE + target},
-                device_id_type=MESH,
-            ).start()
+        pltpu.make_async_remote_copy(
+            src_ref=cross.at[late],
+            dst_ref=visit.at[slot, :, :, piece(place - VIA)],
+            send_sem=pass_send.at[order],
+            recv_sem=visit_recv.at[slot],
+            device_id={"band": side * LINE + target},
+            device_id_type=MESH,
+        ).start()
 
     passes = ((0, 0, 0), (1, 0, 1), (0, 1, 1))
 
@@ -258,14 +254,16 @@
 
     send(0)
     factors()
-    relay(0)
+
+    @pl.when(via)
+    def _():
+        relay(0)
+        relay(1)
+        pass_on(*passes[2], 2)
 
     @pl.when(place > 0)
     def _():
         next_turn(1)
-
-    relay(1)
-    pass_on(*passes[2], 2)
 
     @pl.when(inner)
     def _():
@@ -301,9 +299,9 @@
         def _():
             pltpu.make_async_copy(whole, whole, cross_send.at[late]).wait()
 
-    for order, (late, target, slot) in enumerate(passes):
-        @pl.when(place != target)
-        def _():
+    @pl.when(via)
+    def _():
+        for order, (late, target, slot) in enumerate(passes):
             pltpu.make_async_copy(cross.at[late], cross.at[late], pass_send.at[order]).wait()
 
     for turn in range(TURNS):

time: 75 us -> 72.8 us (0.971)
  Pallas kernels: 73.2 us -> 71 us
    pallas_call x1, Pallas kernels: 73.2 us -> 71 us  [local(): pl.pallas_call(kernel, out_shape=jax.ShapeDtypeStruct((1, 2, N, N), F32),...]
where the time goes in v4:
time: 72.8 us; the launch traced here: 72.6 us
  Pallas kernels  71 us (98%)
  other arithmetic  1.57 us (2%)
    pallas_call x1, Pallas kernels, local(): pl.pallas_call(kernel, out_shape=jax.ShapeDtypeStruct((1, 2, N, N), F32),...  71 us
    mul x1, other arithmetic, local(): return -mix_fraction * total  1.57 us

profile of v4, /device:TPU:1, one launch (start us, length us, event | category | flops | bytes accessed | tf_op | source)
XLA Modules:
  0.0 72.6 jit_solution(13948546901030396909)
XLA Ops:
  0.0 71.0 %shard_map.100 = f32[1,2,128,128]{3,2,1,0:T(8,128)} custom-call(f32[1,2,128,128]{3,2,1,0:T(8,128)} %res.1, f32[2,2,128,128]{3,2,1,0:T(8,128)} %occ.1, bf16[256,256]{1,0:T(8,128)(2,1)} %constant.18.clone.z_high, bf16[256,256]{1,0:T(8,128)(2,1)} %constant.19.clone.z_low, bf16[256,256]{1,0:T(8,128)(2,1)} %constant.20.clone.y_high, ...), custom_call_target="tpu_custom_call" | custom-call | tf_op jit(solution)/shard_map/pallas_call | solution.py:314
  71.0 1.6 %broadcast_multiply_fusion = f32[1,2,128,128]{3,2,1,0:T(8,128)} fusion(f32[1,2,128,128]{3,2,1,0:T(8,128)} %shard_map.100), kind=kLoop, calls=%fused_computation | loop fusion | flops 32768 | bytes 262144 | tf_op jit(solution)/shard_map/mul | solution.py:339
